TPU v7x, 256 devices: a whole 4x4x8 slice. The times are simulated.
256 devices in a mesh: row: 32 (over y, z_lo, core), col: 8 (over x, z_hi).
Axes of the slice: x: 4, y: 4, z: 8 (z_hi: 2, z_lo: 4; z = z_hi * 4 + z_lo), core: 2. Of those that a mesh axis runs over, the one named last changes fastest.
Arguments:
- object_field: bfloat16 [2, 8192, 8192], P(None, 'row', 'col'), may hold values from -6 to 6
- probe: float32 [2, 2, 256, 256], replicated, may hold values from -5 to 5
- measured: bfloat16 [32, 8, 12, 256, 256], P('row', 'col'), may hold values from 0.3984375 to 4
- positions: int32 [32, 8, 12, 2], P('row', 'col'), may hold values from 0 to 1023, as said below
- counts: int32 [32, 8], P('row', 'col'), may hold values from 1 to 12, as said below
Outputs:
- object_grad: float32 [2, 8192, 8192], P(None, 'row', 'col')
- probe_grad: float32 [2, 2, 256, 256], replicated
Inputs may be any that keep to these rules, and one draw needn't show every extreme that they name: positions[i, j, s, 0] lies in 0 to 255 and positions[i, j, s, 1] in 0 to 1023 for every slot, live or not. `counts`: some tile has all 12 slots live.
All inputs are finite; a program needn't handle non-finite values.
Results may differ from a plain program's by a relative error of at most 0.0048.
The roundings to bfloat16 on the way count: a program that leaves them out, or rounds other values in their place, can miss the bound.
Values may be sent and summed in bfloat16 or wider, within the bound.
No kernel may reach another device: no remote copies, remote signals or barrier semaphores. Data moves between devices by JAX's collectives and lax.ppermute only.
A program may use at most 128 MiB of HBM per device.

v0:
```python
import jax
import jax.numpy as jnp
from jax import lax
from jax.sharding import PartitionSpec as P


def from_behind(x, axis, by):
    peers = lax.axis_size(axis)
    pairs = [(i, i + by) for i in range(peers) if 0 <= i + by < peers]
    return lax.ppermute(x, axis, pairs)


def dft_tables(size, sign):
    index = jnp.arange(size, dtype=jnp.int32)
    phase = index[:, None] * index[None, :] % size
    angle = 2.0 * jnp.pi / size * phase.astype(jnp.float32)
    cosine = jnp.cos(angle) / jnp.sqrt(jnp.float32(size))
    sine = sign * jnp.sin(angle) / jnp.sqrt(jnp.float32(size))
    left = jnp.stack([jnp.stack([cosine, sine], 0), jnp.stack([-sine, cosine], 0)], 0)
    right = jnp.stack([jnp.stack([cosine, -sine], 1), jnp.stack([sine, cosine], 1)], 0)
    return (left.astype(jnp.bfloat16), right.astype(jnp.bfloat16))


def transform(field, left, right):
    half = jnp.einsum("ocij,mcjk->moik", left, field, preferred_element_type=jnp.float32).astype(
        jnp.bfloat16
    )
    return jnp.einsum("mcij,cjdk->mdik", half, right, preferred_element_type=jnp.float32)


def position_terms(patch, frame, probe, tables):
    fwd_left, fwd_right, inv_left, inv_right = tables
    obj = patch.astype(jnp.float32)
    obj_re, obj_im = (obj[0], obj[1])
    pro_re, pro_im = (probe[:, 0], probe[:, 1])
    wave = jnp.stack(
        [pro_re * obj_re - pro_im * obj_im, pro_re * obj_im + pro_im * obj_re], 1
    ).astype(jnp.bfloat16)
    spectrum = transform(wave, fwd_left, fwd_right)
    intensity = jnp.sum(spectrum * spectrum, axis=(0, 1))
    amplitude = jnp.sqrt(intensity + 1.0)
    factor = 1.0 - frame.astype(jnp.float32) / amplitude
    weighted = (spectrum * factor).astype(jnp.bfloat16)
    back = transform(weighted, inv_left, inv_right)
    back_re, back_im = (back[:, 0], back[:, 1])
    obj_grad = jnp.stack(
        [
            jnp.sum(pro_re * back_re + pro_im * back_im, 0),
            jnp.sum(pro_re * back_im - pro_im * back_re, 0),
        ],
        0,
    )
    probe_part = jnp.stack(
        [obj_re * back_re + obj_im * back_im, obj_re * back_im - obj_im * back_re], 1
    )
    return (obj_grad, probe_part)


def add_patch(grad, patch, row_at, col_at):
    zero = jnp.zeros((), jnp.int32)
    size = patch.shape[-1]
    old = lax.dynamic_slice(grad, (zero, row_at, col_at), (2, size, size))
    return lax.dynamic_update_slice(grad, old + patch, (zero, row_at, col_at))


def body(object_field, probe, measured, positions, counts):
    size = probe.shape[-1]
    tile_rows = object_field.shape[1]
    tile_cols = object_field.shape[2]
    slots = measured.shape[2]
    frames = measured[0, 0]
    offsets = positions[0, 0]
    count = counts[0, 0]
    fwd_left, fwd_right = dft_tables(size, 1.0)
    inv_left, inv_right = dft_tables(size, -1.0)
    tables = (fwd_left, fwd_right, inv_left, inv_right)
    zero = jnp.zeros((), jnp.int32)
    below = from_behind(object_field, "row", -1)
    tall = jnp.concatenate([object_field, below], 1)
    strip = from_behind(tall[:, :, :size], "col", -1)
    extended = jnp.concatenate([tall, strip], 2)
    grad = jnp.zeros(extended.shape, jnp.float32)
    probe_sum = jnp.zeros(probe.shape, jnp.float32)

    def own_step(index, carry):
        grad_now, probe_now = carry
        row_at = offsets[index, 0]
        col_at = offsets[index, 1]
        patch = lax.dynamic_slice(extended, (zero, row_at, col_at), (2, size, size))
        obj_grad, probe_part = position_terms(patch, frames[index], probe, tables)
        return (add_patch(grad_now, obj_grad, row_at, col_at), probe_now + probe_part)

    grad, probe_sum = lax.fori_loop(0, count, own_step, (grad, probe_sum))
    total_slots = slots * lax.axis_size("row") * lax.axis_size("col")
    probe_grad = lax.psum(probe_sum / jnp.sqrt(jnp.float32(total_slots)), ("row", "col"))
    strip_grad = from_behind(grad[:, :, tile_cols:], "col", 1)
    grad = grad[:, :, :tile_cols]
    grad = grad.at[:, :, :size].add(strip_grad)
    band_grad = from_behind(grad[:, tile_rows:, :], "row", 1)
    grad = grad[:, :tile_rows, :]
    object_grad = grad.at[:, :size, :].add(band_grad)
    return (object_grad, probe_grad)


def solution(mesh):
    placed = (
        P(None, "row", "col"),
        P(),
        P("row", "col", None, None, None),
        P("row", "col", None, None),
        P("row", "col"),
    )
    return jax.shard_map(
        body, mesh=mesh, in_specs=placed, out_specs=(P(None, "row", "col"), P()), check_vma=False
    )
```

profile of v0, /device:TPU:2, one launch (start us, length us, event | category | flops | bytes accessed | tf_op | source)
XLA Modules:
  0.0 633.6 jit_solution(1954523480377900245)
XLA Ops:
  7.2 1.4 collective-permute-start
  15.1 1.3 copy-done.2
  17.3 9.1 %collective-permute-start.1 = (bf16[2,512,256]{2,1,0:T(8,128)(2,1)}, bf16[2,512,256]{2,1,0:T(8,128)(2,1)S(1)}, u32[]{:S(2)}, u32[]{:S(2)}) collective-permute-start(bf16[2,512,256]{2,1,0:T(8,128)(2,1)} %slice.87), channel_id=1, source_target_pairs={{1,0},{2,1},{3,2},{4,3},{5,4},{6,5},{7,6},{9,8},{10,9},{11,10},{12... | collective-permute-start | bytes 1572872 | tf_op jit(solution)/shard_map/ppermute | solution.py:10
  26.3 1.6 negate_convert_fusion.3
  31.2 2.5 collective-permute-done.1
  33.7 1.7 pad_maximum_fusion
  36.4 2.6 broadcast_in_dim.4
  39.1 24.3 %while.15 = (s32[]{:T(128)}, f32[2,512,1280]{2,1,0:T(8,128)}, f32[2,2,256,256]{3,2,1,0:T(8,128)}, s32[]{:T(128)}, s32[12,2]{0,1:T(2,128)S(1)}, /*index=5*/f32[2,...) while((s32[]{:T(128)}, f32[2,512,1280]{2,1,0:T(8,128)}, ...), condition=%wide.region_4.5_spmd, body=%wide.region_0.4_spmd.sunk | while | flops 1080229888 | bytes 25035120 | solution.py:93
  46.1 2.8 multiply_reduce_fusion.2
  49.8 2.1 convolution_bitcast_fusion.5
  52.2 1.4 maximum_add_fusion.4
  53.7 2.3 maximum_add_fusion.5
  56.0 6.8 %dynamic_update_slice.4 = f32[2,512,1280]{2,1,0:T(8,128)} dynamic-update-slice(f32[2,512,1280]{2,1,0:T(8,128)} %get-tuple-element.280, f32[2,256,256]{2,1,0:T(8,128)S(1)} %maximum_add_fusion.4, s32[]{:T(128)} %constant.104.clone.1..sunk, s32[]{:T(128)S(6)} %select_n.140, s32[]{:T(128)S(6)} %select_n.141) | dynamic-update-slice | bytes 1048580 | tf_op jit(solution)/shard_map/while/body/dynamic_update_slice | solution.py:63
  64.7 100.0 %collective-permute-start.2 = (f32[2,512,256]{2,1,0:T(8,128)S(1)}, f32[2,512,256]{2,1,0:T(8,128)S(1)}, u32[]{:S(2)}, u32[]{:S(2)}) collective-permute-start(f32[2,512,256]{2,1,0:T(8,128)S(1)} %slice.80), channel_id=1, source_target_pairs={{0,1},{1,2},{2,3},{3,4},{4,5},{5,6},{6,7},{8,9},{9,10},{10,11},{11... | collective-permute-start | bytes 3145736 | tf_op jit(solution)/shard_map/ppermute | solution.py:10
  164.8 2.5 slice.78
  167.3 46.9 %collective-permute-done.2 = f32[2,512,256]{2,1,0:T(8,128)S(1)} collective-permute-done((f32[2,512,256]{2,1,0:T(8,128)S(1)}, f32[2,512,256]{2,1,0:T(8,128)S(1)}, u32[]{:S(2)}, u32[]{:S(2)}) %collective-permute-start.2) | collective-permute-done | bytes 1048608 | tf_op jit(solution)/shard_map/ppermute | solution.py:10
  214.2 1.4 add_dynamic-update-slice_fusion
  215.6 1.9 copy-done.1
  217.5 1.5 slice.89
  219.0 2.6 collective-permute-start.3
  221.6 2.3 broadcast_multiply_fusion
  224.4 4.1 slice_add_fusion
  228.5 396.0 %all-reduce.2.cloned.1.call-done = f32[2,2,256,256]{3,2,1,0:T(8,128)} async-done(((f32[2,2,256,256]{3,2,1,0:T(8,128)}), f32[2,2,256,256]{3,2,1,0:T(8,128)}) %all-reduce.2.cloned.1.call-update) | async-done | bytes 1048592 | tf_op jit(solution)/shard_map/psum | solution.py:95
  624.5 2.3 copy.30
  (42 shorter events, 16.6 us)
Async XLA Ops:
  7.2 7.7 %copy-start.4 = (bf16[2,256,1024]{2,1,0:T(8,128)(2,1)S(1)}, bf16[2,256,1024]{2,1,0:T(8,128)(2,1)}, u32[]{:S(2)}) copy-start(bf16[2,256,1024]{2,1,0:T(8,128)(2,1)} %param.13) | copy-start | bytes 3145732
  7.2 617.3 %all-reduce.2.cloned.1.call-start = ((), (), s32[]{:S(2)}) async-start(), calls=%async_computation | async-start | bytes 2097152 | tf_op jit(solution)/shard_map/psum | solution.py:95
  7.2 7.8 %collective-permute-start = (bf16[2,256,1024]{2,1,0:T(8,128)(2,1)}, bf16[2,256,1024]{2,1,0:T(8,128)(2,1)S(1)}, u32[]{:S(2)}, u32[]{:S(2)}) collective-permute-start(bf16[2,256,1024]{2,1,0:T(8,128)(2,1)} %param.13), channel_id=1, source_target_pairs={{8,0},{16,8},{24,16},{32,24},{40,32},{48,40},{56,48},{64,56},{72,6... | collective-permute-start | bytes 3145736 | tf_op jit(solution)/shard_map/ppermute | solution.py:10
  15.1 1.3 copy-start.2
  17.3 16.4 %collective-permute-start.1 = (bf16[2,512,256]{2,1,0:T(8,128)(2,1)}, bf16[2,512,256]{2,1,0:T(8,128)(2,1)S(1)}, u32[]{:S(2)}, u32[]{:S(2)}) collective-permute-start(bf16[2,512,256]{2,1,0:T(8,128)(2,1)} %slice.87), channel_id=1, source_target_pairs={{1,0},{2,1},{3,2},{4,3},{5,4},{6,5},{7,6},{9,8},{10,9},{11,10},{12... | collective-permute-start | bytes 1572872 | tf_op jit(solution)/shard_map/ppermute | solution.py:10
  28.0 5.7 copy-start.3
  36.4 2.7 copy-start
  36.4 2.7 copy-start.7
  39.9 9.0 %copy-start.5 = (bf16[2,256,2,256]{3,1,0,2:T(8,128)(2,1)}, bf16[2,256,2,256]{3,1,0,2:T(8,128)(2,1)S(1)}, u32[]{:S(2)}) copy-start(bf16[2,256,2,256]{3,1,0,2:T(8,128)(2,1)S(1)} %get-tuple-element.304) | copy-start | bytes 1572868 | tf_op jit(solution)/shard_map/while
  52.2 10.6 %copy-start.6 = (bf16[2,256,2,256]{3,1,0,2:T(8,128)(2,1)S(1)}, bf16[2,256,2,256]{3,1,0,2:T(8,128)(2,1)}, u32[]{:S(2)}) copy-start(bf16[2,256,2,256]{3,1,0,2:T(8,128)(2,1)} %copy-done.5) | copy-start | bytes 1572868 | tf_op jit(solution)/shard_map/while
  64.7 149.4 %collective-permute-start.2 = (f32[2,512,256]{2,1,0:T(8,128)S(1)}, f32[2,512,256]{2,1,0:T(8,128)S(1)}, u32[]{:S(2)}, u32[]{:S(2)}) collective-permute-start(f32[2,512,256]{2,1,0:T(8,128)S(1)} %slice.80), channel_id=1, source_target_pairs={{0,1},{1,2},{2,3},{3,4},{4,5},{5,6},{6,7},{8,9},{9,10},{10,11},{11... | collective-permute-start | bytes 3145736 | tf_op jit(solution)/shard_map/ppermute | solution.py:10
  215.6 1.9 copy-start.1
  219.0 5.4 collective-permute-start.3
Sparse Core Ops, SparseCore 0:
  224.1 400.3 all-reduce.1
where the time goes:
time: 639 us; the launch traced here: 634 us
  waiting for transfers between devices  446 us (70%)
  starting transfers between devices  113 us (18%)
  other arithmetic  26.8 us (4%)
  local copies, waits for them, and re-layouts  23.1 us (4%)
  between operations  14.2 us (2%)
    psum x1, waiting for transfers between devices, body(): lax.psum(probe_sum / jnp.sqrt(jnp.float32(total_slots)), ('row', 'col'))  396 us
    ppermute x4, starting transfers between devices, from_behind(): return lax.ppermute(x, axis, pairs)  113 us
    ppermute x4, waiting for transfers between devices, from_behind(): return lax.ppermute(x, axis, pairs)  49.8 us
  transfers between devices with their start and end apart: 5, of which 4 were waited for; matrix products, arithmetic and copies ran while one was open for 3% of the time, Pallas kernels for 0%

commit v1 on v0

--- a/solution.py
+++ b/solution.py
@@ -92,7 +92,7 @@
 
     grad, probe_sum = lax.fori_loop(0, count, own_step, (grad, probe_sum))
     total_slots = slots * lax.axis_size("row") * lax.axis_size("col")
-    probe_grad = lax.psum(probe_sum / jnp.sqrt(jnp.float32(total_slots)), ("row", "col"))
+    probe_grad = lax.psum(lax.psum(probe_sum / jnp.sqrt(jnp.float32(total_slots)), "col"), "row")
     strip_grad = from_behind(grad[:, :, tile_cols:], "col", 1)
     grad = grad[:, :, :tile_cols]
     grad = grad.at[:, :, :size].add(strip_grad)

time: 639 us -> 800 us (1.25)
  waiting for transfers between devices: 446 us -> 608 us
    psum x1 -> x2, waiting for transfers between devices: 396 us -> 560 us  [the longest x1 282 us: body(): lax.psum(probe_sum / jnp.sqrt(jnp.float32(total_slots)), 'col')]
  transfers between devices with their start and end apart: 5 -> 6, of which waited for: 4 -> 4; matrix products, arithmetic and copies ran while one was open for 3% -> 3% of each run, Pallas kernels for 0% -> 0%
where the time goes in v1:
time: 800 us; the launch traced here: 793 us
  waiting for transfers between devices  608 us (76%)
  starting transfers between devices  111 us (14%)
  other arithmetic  27.1 us (3%)
  local copies, waits for them, and re-layouts  22.5 us (3%)
  between operations  14.2 us (2%)
    psum x1, waiting for transfers between devices, body(): lax.psum(probe_sum / jnp.sqrt(jnp.float32(total_slots)), 'col')  282 us
    psum x1, waiting for transfers between devices, body(): lax.psum(lax.psum(probe_sum / jnp.sqrt(jnp.float32(total_slots)), 'col'),...  278 us
    ppermute x4, starting transfers between devices, from_behind(): return lax.ppermute(x, axis, pairs)  111 us
    ppermute x4, waiting for transfers between devices, from_behind(): return lax.ppermute(x, axis, pairs)  48.4 us
  transfers between devices with their start and end apart: 6, of which 4 were waited for; matrix products, arithmetic and copies ran while one was open for 3% of the time, Pallas kernels for 0%

profile of v1, /device:TPU:2, one launch (start us, length us, event | category | flops | bytes accessed | tf_op | source)
XLA Modules:
  0.0 792.8 jit_solution(5354849973903325964)
XLA Ops:
  7.2 1.4 collective-permute-start
  15.9 9.1 %collective-permute-start.1 = (bf16[2,512,256]{2,1,0:T(8,128)(2,1)}, bf16[2,512,256]{2,1,0:T(8,128)(2,1)}, u32[]{:S(2)}, u32[]{:S(2)}) collective-permute-start(bf16[2,512,256]{2,1,0:T(8,128)(2,1)} %slice.87), channel_id=1, source_target_pairs={{1,0},{2,1},{3,2},{4,3},{5,4},{6,5},{7,6},{9,8},{10,9},{11,10},{12... | collective-permute-start | bytes 1572872 | tf_op jit(solution)/shard_map/ppermute | solution.py:10
  25.0 1.7 negate_convert_fusion.3
  30.7 1.8 collective-permute-done.1
  32.5 2.7 pad_maximum_fusion
  36.3 2.6 broadcast_in_dim.4
  38.9 24.0 %while.15 = (s32[]{:T(128)}, f32[2,512,1280]{2,1,0:T(8,128)}, f32[2,2,256,256]{3,2,1,0:T(8,128)}, s32[]{:T(128)}, s32[12,2]{0,1:T(2,128)S(1)}, /*index=5*/f32[2,...) while((s32[]{:T(128)}, f32[2,512,1280]{2,1,0:T(8,128)}, ...), condition=%wide.region_4.5_spmd, body=%wide.region_0.4_spmd.sunk | while | flops 1080229888 | bytes 22937948 | solution.py:93
  45.6 2.8 multiply_reduce_fusion.2
  49.4 2.1 convolution_bitcast_fusion.5
  51.7 1.4 maximum_add_fusion.4
  53.2 2.3 maximum_add_fusion.5
  55.5 6.8 dynamic_update_slice.4
  64.2 98.8 %collective-permute-start.2 = (f32[2,512,256]{2,1,0:T(8,128)S(1)}, f32[2,512,256]{2,1,0:T(8,128)S(1)}, u32[]{:S(2)}, u32[]{:S(2)}) collective-permute-start(f32[2,512,256]{2,1,0:T(8,128)S(1)} %slice.80), channel_id=1, source_target_pairs={{0,1},{1,2},{2,3},{3,4},{4,5},{5,6},{6,7},{8,9},{9,10},{10,11},{11... | collective-permute-start | bytes 3145736 | tf_op jit(solution)/shard_map/ppermute | solution.py:10
  163.0 2.5 slice.78
  165.6 46.6 %collective-permute-done.2 = f32[2,512,256]{2,1,0:T(8,128)S(1)} collective-permute-done((f32[2,512,256]{2,1,0:T(8,128)S(1)}, f32[2,512,256]{2,1,0:T(8,128)S(1)}, u32[]{:S(2)}, u32[]{:S(2)}) %collective-permute-start.2) | collective-permute-done | bytes 1048608 | tf_op jit(solution)/shard_map/ppermute | solution.py:10
  212.2 1.4 add_dynamic-update-slice_fusion
  213.6 1.9 copy-done.1
  215.5 1.5 slice.89
  217.0 1.4 collective-permute-start.3
  218.4 2.3 broadcast_multiply_fusion
  220.8 281.9 %all-reduce.3.cloned.1.call-done = f32[2,2,256,256]{3,2,1,0:T(8,128)} async-done(((f32[2,2,256,256]{3,2,1,0:T(8,128)}), f32[2,2,256,256]{3,2,1,0:T(8,128)}) %all-reduce.3.cloned.1.call-update) | async-done | bytes 1048592 | tf_op jit(solution)/shard_map/psum | solution.py:95
  502.7 3.3 slice_add_fusion
  506.0 277.6 %all-reduce.5.cloned.1.call-done = f32[2,2,256,256]{3,2,1,0:T(8,128)} async-done(((f32[2,2,256,256]{3,2,1,0:T(8,128)}), f32[2,2,256,256]{3,2,1,0:T(8,128)}) %all-reduce.5.cloned.1.call-update) | async-done | bytes 1048592 | tf_op jit(solution)/shard_map/psum | solution.py:95
  783.6 2.3 copy.31
  (41 shorter events, 17.0 us)
Async XLA Ops:
  7.2 495.5 %all-reduce.3.cloned.1.call-start = ((), (), s32[]{:S(2)}) async-start(), calls=%async_computation | async-start | bytes 2097152 | tf_op jit(solution)/shard_map/psum | solution.py:95
  7.2 7.7 copy-start.2
  7.2 7.8 collective-permute-start
  15.9 16.6 %collective-permute-start.1 = (bf16[2,512,256]{2,1,0:T(8,128)(2,1)}, bf16[2,512,256]{2,1,0:T(8,128)(2,1)}, u32[]{:S(2)}, u32[]{:S(2)}) collective-permute-start(bf16[2,512,256]{2,1,0:T(8,128)(2,1)} %slice.87), channel_id=1, source_target_pairs={{1,0},{2,1},{3,2},{4,3},{5,4},{6,5},{7,6},{9,8},{10,9},{11,10},{12... | collective-permute-start | bytes 1572872 | tf_op jit(solution)/shard_map/ppermute | solution.py:10
  36.3 2.7 copy-start
  36.3 2.7 copy-start.3
  36.3 2.7 copy-start.5
  51.7 10.5 %copy-start.4 = (bf16[2,256,2,256]{3,1,0,2:T(8,128)(2,1)S(1)}, bf16[2,256,2,256]{3,1,0,2:T(8,128)(2,1)}, u32[]{:S(2)}) copy-start(bf16[2,256,2,256]{3,1,0,2:T(8,128)(2,1)} %get-tuple-element.345) | copy-start | bytes 1572868 | tf_op jit(solution)/shard_map/while
  64.2 148.0 %collective-permute-start.2 = (f32[2,512,256]{2,1,0:T(8,128)S(1)}, f32[2,512,256]{2,1,0:T(8,128)S(1)}, u32[]{:S(2)}, u32[]{:S(2)}) collective-permute-start(f32[2,512,256]{2,1,0:T(8,128)S(1)} %slice.80), channel_id=1, source_target_pairs={{0,1},{1,2},{2,3},{3,4},{4,5},{5,6},{6,7},{8,9},{9,10},{10,11},{11... | collective-permute-start | bytes 3145736 | tf_op jit(solution)/shard_map/ppermute | solution.py:10
  213.6 2.0 copy-start.1
  217.0 285.7 %collective-permute-start.3 = (f32[2,256,1024]{2,1,0:T(8,128)}, f32[2,256,1024]{2,1,0:T(8,128)S(1)}, u32[]{:S(2)}, u32[]{:S(2)}) collective-permute-start(f32[2,256,1024]{2,1,0:T(8,128)} %slice.89), channel_id=1, source_target_pairs={{0,8},{8,16},{16,24},{24,32},{32,40},{40,48},{48,56},{56,64},{64,7... | collective-permute-start | bytes 6291464 | tf_op jit(solution)/shard_map/ppermute | solution.py:10
  220.8 562.9 %all-reduce.5.cloned.1.call-start = ((), (), s32[]{:S(2)}) async-start(), calls=%async_computation.1 | async-start | bytes 2097152 | tf_op jit(solution)/shard_map/psum | solution.py:95
Sparse Core Ops, SparseCore 0:
  220.9 281.7 all-reduce.2
  505.3 278.3 all-reduce.4
